TPU v7x, 128 devices: a whole 4x4x4 slice. The times are simulated.
128 devices in a mesh: ka: 4 (over x_hi, core), brick: 32 (over z, x_lo, y).
Axes of the slice: x: 4 (x_hi: 2, x_lo: 2; x = x_hi * 2 + x_lo), y: 4, z: 4, core: 2. Of those that a mesh axis runs over, the one named last changes fastest.
Arguments:
- spinors: bfloat16 [32, 4, 128, 36864], P('ka', None, 'brick'), may hold values from -6 to 6
- kpt_mult: int32 [32], P('ka'), may hold values from 1 to 4
- occupied: int32 [32], P('ka'), may hold values 0 or 1
- core_density: float32 [128, 36864], P('brick'), may hold values from 0.05 to 1
- local_potential: float32 [128, 36864], P('brick'), may hold values from -6 to 6
Outputs:
- applied: bfloat16 [32, 4, 128, 36864], P('ka', None, 'brick')
All inputs are finite; a program needn't handle non-finite values. No bound on the sum of `occupied` on one device may be relied on, other than what follows from the above.
Results may differ from a plain program's by a relative error of at most 0.005.
Values may be sent and summed in bfloat16 or wider, within the bound.
A program may use at most 128 MiB of HBM per device.

v0:
```python
import math

import jax
import jax.numpy as jnp
from jax import lax
from jax.sharding import PartitionSpec as P

NY = 192


FLOOR_FRACTION = 0.05


def with_halo(x, sides, width):
    for axis, dim in sides:
        size, length = (lax.axis_size(axis), x.shape[dim])
        up = [(i, (i + 1) % size) for i in range(size - 1)]
        down = [(j, i) for i, j in up]
        last = lax.slice_in_dim(x, length - width, length, axis=dim)
        initial = lax.slice_in_dim(x, 0, width, axis=dim)
        before = lax.ppermute(last, axis, up)
        after = lax.ppermute(initial, axis, down)
        x = jnp.concatenate([before, x, after], axis=dim)
    return x


def density_terms(band, weight):
    values = band.astype(jnp.float32)
    up_real, up_imag, down_real, down_imag = (values[0], values[1], values[2], values[3])
    up_square = up_real * up_real + up_imag * up_imag
    down_square = down_real * down_real + down_imag * down_imag
    return weight * jnp.stack(
        [
            up_square + down_square,
            2.0 * (up_real * down_real + up_imag * down_imag),
            2.0 * (up_real * down_imag - up_imag * down_real),
            up_square - down_square,
        ]
    )


def accumulate_density(spinors, weights):
    zeros = jnp.zeros((4,) + spinors.shape[2:], jnp.float32)

    def step_band(carry, item):
        band, weight = item
        return (carry + density_terms(band, weight), None)

    result, unused = lax.scan(step_band, zeros, (spinors, weights))
    return result


def frame_potential(density, core):
    electrons = density[0] + core
    magnitude = jnp.sqrt(
        density[1] * density[1] + density[2] * density[2] + density[3] * density[3]
    )
    upper = -jnp.cbrt(3.0 / math.pi * (electrons + magnitude))
    lower = -jnp.cbrt(3.0 / math.pi * (electrons - magnitude))
    factor = 0.5 * (upper - lower) / jnp.maximum(magnitude, FLOOR_FRACTION * electrons)
    return jnp.stack(
        [0.5 * (upper + lower), factor * density[1], factor * density[2], factor * density[3]]
    )


def plane_neighbours(center, row_length):
    column = jnp.arange(center.shape[-1], dtype=jnp.int32) % row_length
    forward = jnp.where(
        column == row_length - 1, jnp.roll(center, row_length - 1, -1), jnp.roll(center, -1, -1)
    )
    backward = jnp.where(column == 0, jnp.roll(center, 1 - row_length, -1), jnp.roll(center, 1, -1))
    across = jnp.roll(center, row_length, -1) + jnp.roll(center, -row_length, -1)
    return forward + backward + across


def apply_hamiltonian(padded_band, potential):
    values = padded_band.astype(jnp.float32)
    center = values[:, 1:-1]
    neighbours = values[:, 2:] + values[:, :-2]
    neighbours = neighbours + plane_neighbours(center, NY)
    kinetic = -0.5 * (neighbours - 6.0 * center)
    diagonal_up = potential[0] + potential[3]
    diagonal_down = potential[0] - potential[3]
    field_x, field_y = (potential[1], potential[2])
    up_real, up_imag, down_real, down_imag = (center[0], center[1], center[2], center[3])
    mixed = jnp.stack(
        [
            diagonal_up * up_real + field_x * down_real + field_y * down_imag,
            diagonal_up * up_imag + field_x * down_imag - field_y * down_real,
            field_x * up_real - field_y * up_imag + diagonal_down * down_real,
            field_x * up_imag + field_y * up_real + diagonal_down * down_imag,
        ]
    )
    return (kinetic + mixed).astype(jnp.bfloat16)


def apply_bands(padded_bands, potential):

    def one_band(band):
        return apply_hamiltonian(band, potential)

    return lax.map(one_band, padded_bands)


def shards(spinors, kpt_mult, occupied, core_density, local_potential):
    band_count = spinors.shape[0]
    band_total = band_count * lax.axis_size("ka")
    weights = (kpt_mult * occupied).astype(jnp.float32) / (2.0 * band_total)
    density = accumulate_density(spinors, weights)
    summed = lax.psum(density.astype(jnp.bfloat16), "ka").astype(jnp.float32)
    potential = frame_potential(summed, core_density)
    potential = jnp.concatenate([(potential[0] + local_potential)[None], potential[1:]], axis=0)
    padded = with_halo(spinors, (("brick", 2),), 1)
    return apply_bands(padded, potential)


def solution(mesh):
    placed = (P("ka", None, "brick", None), P("ka"), P("ka"), P("brick", None), P("brick", None))
    return jax.shard_map(
        shards, mesh=mesh, in_specs=placed, out_specs=P("ka", None, "brick", None), check_vma=False
    )
```

profile of v0, /device:TPU:96, one launch (start us, length us, event | category | flops | bytes accessed | tf_op | source)
XLA Modules:
  0.0 341.6 jit_solution(15574771196927574068)
XLA Ops:
  7.2 52.5 %while.25 = (s32[]{:T(128)}, f32[4,4,36864]{2,1,0:T(4,128)S(1)}, f32[8]{0:T(128)S(1)}, bf16[8,4,4,36864]{3,2,1,0:T(4,128)(2,1)}, s32[]{:T(128)}, /*index=5*/s32[]{:T(128)}) while((s32[]{:T(128)}, f32[4,4,36864]{2,1,0:T(4,128)S(1)}, f32[8]{0:T(128)S(1)}, bf16[8,4,4,36864]{3,2,1,0:T(4,128)(2,1)}, s32[]{:T(128)}, ...), condition=%wide.region_1.2_spmd.clone, body=%wide.region_0.1_spmd.clone.sunk | while | flops 6488067 | bytes 15335523 | solution.py:49
  10.9 2.8 fusion.49
  17.5 2.8 fusion.49
  24.0 2.8 fusion.49
  30.6 2.8 fusion.49
  37.2 2.8 fusion.49
  43.7 2.8 fusion.49
  50.3 2.8 fusion.49
  56.9 2.8 fusion.49
  61.2 12.5 %fusion.31 = (bf16[8,4,1,36864]{3,2,1,0:T(2,128)(2,1)S(1)}, bf16[8,4,1,36864]{3,2,1,0:T(2,128)(2,1)S(1)}) fusion(bf16[8,4,4,36864]{3,2,1,0:T(4,128)(2,1)} %get-tuple-element.376), kind=kLoop, calls=%fused_computation.69 | loop fusion | bytes 9437184 | tf_op jit(solution)/shard_map/slice | solution.py:19
  73.7 4.0 %copy.10 = bf16[8,4,1,36864]{3,0,2,1:T(8,128)(2,1)} copy(bf16[8,4,1,36864]{3,2,1,0:T(2,128)(2,1)S(1)} %get-tuple-element.216) | data formatting | bytes 4718592
  77.7 3.5 %collective-permute-start = (bf16[8,4,1,36864]{3,0,2,1:T(8,128)(2,1)}, bf16[8,4,1,36864]{3,0,2,1:T(8,128)(2,1)}, u32[]{:S(2)}, u32[]{:S(2)}) collective-permute-start(bf16[8,4,1,36864]{3,0,2,1:T(8,128)(2,1)} %copy.10), channel_id=1, source_target_pairs={{0,1},{1,2},{2,3},{3,4},{4,5},{5,6},{6,7},{7,8},{8,9},{9,10},{10,1... | collective-permute-start | bytes 7077896 | tf_op jit(solution)/shard_map/ppermute | solution.py:21
  81.2 4.0 %copy.11 = bf16[8,4,1,36864]{3,0,2,1:T(8,128)(2,1)} copy(bf16[8,4,1,36864]{3,2,1,0:T(2,128)(2,1)S(1)} %get-tuple-element.217) | data formatting | bytes 4718592
  85.2 5.7 %collective-permute-start.1 = (bf16[8,4,1,36864]{3,0,2,1:T(8,128)(2,1)}, bf16[8,4,1,36864]{3,0,2,1:T(8,128)(2,1)}, u32[]{:S(2)}, u32[]{:S(2)}) collective-permute-start(bf16[8,4,1,36864]{3,0,2,1:T(8,128)(2,1)} %copy.11), channel_id=1, source_target_pairs={{1,0},{2,1},{3,2},{4,3},{5,4},{6,5},{7,6},{8,7},{9,8},{10,9},{11,1... | collective-permute-start | bytes 7077896 | tf_op jit(solution)/shard_map/ppermute | solution.py:22
  90.9 28.3 %all-reduce.2.cloned.1.call-done = bf16[4,4,36864]{2,1,0:T(4,128)(2,1)} async-done(((bf16[4,4,36864]{2,1,0:T(4,128)(2,1)}), bf16[4,4,36864]{2,1,0:T(4,128)(2,1)}) %all-reduce.2.cloned.1.call-update) | async-done | bytes 1179664 | tf_op jit(solution)/shard_map/psum | solution.py:110
  120.6 2.9 subtract_bitcast_fusion.1
  123.9 22.7 %collective-permute-done = bf16[8,4,1,36864]{3,0,2,1:T(8,128)(2,1)} collective-permute-done((bf16[8,4,1,36864]{3,0,2,1:T(8,128)(2,1)}, bf16[8,4,1,36864]{3,0,2,1:T(8,128)(2,1)}, u32[]{:S(2)}, u32[]{:S(2)}) %collective-permute-start) | collective-permute-done | bytes 2359328 | tf_op jit(solution)/shard_map/ppermute | solution.py:21
  146.6 8.9 %copy.8 = bf16[8,4,1,36864]{3,2,1,0:T(2,128)(2,1)} copy(bf16[8,4,1,36864]{3,0,2,1:T(8,128)(2,1)} %collective-permute-done) | data formatting | bytes 4718592 | tf_op jit(solution)/shard_map/ppermute | solution.py:21
  155.5 8.9 %copy.9 = bf16[8,4,1,36864]{3,2,1,0:T(2,128)(2,1)} copy(bf16[8,4,1,36864]{3,0,2,1:T(8,128)(2,1)} %collective-permute-done.1) | data formatting | bytes 4718592 | tf_op jit(solution)/shard_map/ppermute | solution.py:22
  164.4 20.7 %pad_maximum_fusion = bf16[8,4,6,36864]{3,2,1,0:T(8,128)(2,1)} fusion(bf16[8,4,1,36864]{3,2,1,0:T(2,128)(2,1)} %copy.9, bf16[8,4,4,36864]{3,2,1,0:T(4,128)(2,1)} %get-tuple-element.376, bf16[8,4,1,36864]{3,2,1,0:T(2,128)(2,1)} %copy.8), kind=kLoop, calls=%fused_computation.46 | loop fusion | flops 42467328 | bytes 28311552 | tf_op jit(solution)/shard_map/concatenate | solution.py:23
  185.1 149.6 %while.24 = (s32[]{:T(128)}, bf16[8,4,4,36864]{3,2,1,0:T(4,128)(2,1)}, bf16[8,4,6,36864]{3,2,1,0:T(8,128)(2,1)}, f32[1,4,36864]{2,1,0:T(4,128)S(1)}, f32[4,36864...) while((s32[]{:T(128)}, bf16[8,4,4,36864]{3,2,1,0:T(4,128)(2,1)}, ...), condition=%wide.region_4.5_spmd, body=%wide.region_3.4_spmd.sunk | while | flops 16515074 | bytes 65618520 | solution.py:102
  185.1 2.0 bitcast_convert_fusion.2
  188.2 1.8 fusion.44
  190.0 1.8 fusion.43
  194.0 9.8 %bitcast_dynamic-update-slice_fusion.2 = bf16[8,4,4,36864]{3,2,1,0:T(4,128)(2,1)} fusion(bf16[8,4,4,36864]{3,2,1,0:T(4,128)(2,1)} %get-tuple-element.360, s32[]{:T(128)} %get-tuple-element.359, f32[1,4,36864]{2,1,0:T(4,128)S(1)} %get-tuple-element.307, f32[1,4,36864]{2,1,0:T(4,128)S(1)} %get-tuple-element.308, ...), kind=kLoop, calls=%fused_computation.13.clone.1 | loop fusion | flops 12386304 | bytes 24846848 | tf_op jit(solution)/shard_map/while/body/jit(dynamic_update_index_in_dim)/dynamic_update_slice | solution.py:102
  203.8 2.0 bitcast_convert_fusion.2
  206.9 1.8 fusion.44
  208.7 1.8 fusion.43
  212.7 9.8 %bitcast_dynamic-update-slice_fusion.2 = bf16[8,4,4,36864]{3,2,1,0:T(4,128)(2,1)} fusion(bf16[8,4,4,36864]{3,2,1,0:T(4,128)(2,1)} %get-tuple-element.360, s32[]{:T(128)} %get-tuple-element.359, f32[1,4,36864]{2,1,0:T(4,128)S(1)} %get-tuple-element.307, f32[1,4,36864]{2,1,0:T(4,128)S(1)} %get-tuple-element.308, ...), kind=kLoop, calls=%fused_computation.13.clone.1 | loop fusion | flops 12386304 | bytes 24846848 | tf_op jit(solution)/shard_map/while/body/jit(dynamic_update_index_in_dim)/dynamic_update_slice | solution.py:102
  222.5 2.0 bitcast_convert_fusion.2
  225.6 1.8 fusion.44
  227.4 1.8 fusion.43
  231.4 9.8 %bitcast_dynamic-update-slice_fusion.2 = bf16[8,4,4,36864]{3,2,1,0:T(4,128)(2,1)} fusion(bf16[8,4,4,36864]{3,2,1,0:T(4,128)(2,1)} %get-tuple-element.360, s32[]{:T(128)} %get-tuple-element.359, f32[1,4,36864]{2,1,0:T(4,128)S(1)} %get-tuple-element.307, f32[1,4,36864]{2,1,0:T(4,128)S(1)} %get-tuple-element.308, ...), kind=kLoop, calls=%fused_computation.13.clone.1 | loop fusion | flops 12386304 | bytes 24846848 | tf_op jit(solution)/shard_map/while/body/jit(dynamic_update_index_in_dim)/dynamic_update_slice | solution.py:102
  241.2 2.0 bitcast_convert_fusion.2
  244.3 1.8 fusion.44
  250.1 9.8 %bitcast_dynamic-update-slice_fusion.2 = bf16[8,4,4,36864]{3,2,1,0:T(4,128)(2,1)} fusion(bf16[8,4,4,36864]{3,2,1,0:T(4,128)(2,1)} %get-tuple-element.360, s32[]{:T(128)} %get-tuple-element.359, f32[1,4,36864]{2,1,0:T(4,128)S(1)} %get-tuple-element.307, f32[1,4,36864]{2,1,0:T(4,128)S(1)} %get-tuple-element.308, ...), kind=kLoop, calls=%fused_computation.13.clone.1 | loop fusion | flops 12386304 | bytes 24846848 | tf_op jit(solution)/shard_map/while/body/jit(dynamic_update_index_in_dim)/dynamic_update_slice | solution.py:102
  259.9 2.0 bitcast_convert_fusion.2
  263.0 1.8 fusion.44
  268.8 9.8 %bitcast_dynamic-update-slice_fusion.2 = bf16[8,4,4,36864]{3,2,1,0:T(4,128)(2,1)} fusion(bf16[8,4,4,36864]{3,2,1,0:T(4,128)(2,1)} %get-tuple-element.360, s32[]{:T(128)} %get-tuple-element.359, f32[1,4,36864]{2,1,0:T(4,128)S(1)} %get-tuple-element.307, f32[1,4,36864]{2,1,0:T(4,128)S(1)} %get-tuple-element.308, ...), kind=kLoop, calls=%fused_computation.13.clone.1 | loop fusion | flops 12386304 | bytes 24846848 | tf_op jit(solution)/shard_map/while/body/jit(dynamic_update_index_in_dim)/dynamic_update_slice | solution.py:102
  278.6 2.0 bitcast_convert_fusion.2
  281.7 1.8 fusion.44
  287.5 9.8 %bitcast_dynamic-update-slice_fusion.2 = bf16[8,4,4,36864]{3,2,1,0:T(4,128)(2,1)} fusion(bf16[8,4,4,36864]{3,2,1,0:T(4,128)(2,1)} %get-tuple-element.360, s32[]{:T(128)} %get-tuple-element.359, f32[1,4,36864]{2,1,0:T(4,128)S(1)} %get-tuple-element.307, f32[1,4,36864]{2,1,0:T(4,128)S(1)} %get-tuple-element.308, ...), kind=kLoop, calls=%fused_computation.13.clone.1 | loop fusion | flops 12386304 | bytes 24846848 | tf_op jit(solution)/shard_map/while/body/jit(dynamic_update_index_in_dim)/dynamic_update_slice | solution.py:102
  297.3 2.0 bitcast_convert_fusion.2
  300.4 1.8 fusion.44
  306.2 9.8 %bitcast_dynamic-update-slice_fusion.2 = bf16[8,4,4,36864]{3,2,1,0:T(4,128)(2,1)} fusion(bf16[8,4,4,36864]{3,2,1,0:T(4,128)(2,1)} %get-tuple-element.360, s32[]{:T(128)} %get-tuple-element.359, f32[1,4,36864]{2,1,0:T(4,128)S(1)} %get-tuple-element.307, f32[1,4,36864]{2,1,0:T(4,128)S(1)} %get-tuple-element.308, ...), kind=kLoop, calls=%fused_computation.13.clone.1 | loop fusion | flops 12386304 | bytes 24846848 | tf_op jit(solution)/shard_map/while/body/jit(dynamic_update_index_in_dim)/dynamic_update_slice | solution.py:102
  316.0 2.0 bitcast_convert_fusion.2
  319.1 1.8 fusion.44
  324.9 9.8 %bitcast_dynamic-update-slice_fusion.2 = bf16[8,4,4,36864]{3,2,1,0:T(4,128)(2,1)} fusion(bf16[8,4,4,36864]{3,2,1,0:T(4,128)(2,1)} %get-tuple-element.360, s32[]{:T(128)} %get-tuple-element.359, f32[1,4,36864]{2,1,0:T(4,128)S(1)} %get-tuple-element.307, f32[1,4,36864]{2,1,0:T(4,128)S(1)} %get-tuple-element.308, ...), kind=kLoop, calls=%fused_computation.13.clone.1 | loop fusion | flops 12386304 | bytes 24846848 | tf_op jit(solution)/shard_map/while/body/jit(dynamic_update_index_in_dim)/dynamic_update_slice | solution.py:102
  (90 shorter events, 68.4 us)
Async XLA Ops:
  6.5 112.6 %all-reduce.2.cloned.1.call-start = ((), (), s32[]{:S(2)}) async-start(), calls=%async_computation | async-start | bytes 2359296 | tf_op jit(solution)/shard_map/psum | solution.py:110
  77.7 68.9 %collective-permute-start = (bf16[8,4,1,36864]{3,0,2,1:T(8,128)(2,1)}, bf16[8,4,1,36864]{3,0,2,1:T(8,128)(2,1)}, u32[]{:S(2)}, u32[]{:S(2)}) collective-permute-start(bf16[8,4,1,36864]{3,0,2,1:T(8,128)(2,1)} %copy.10), channel_id=1, source_target_pairs={{0,1},{1,2},{2,3},{3,4},{4,5},{5,6},{6,7},{7,8},{8,9},{9,10},{10,1... | collective-permute-start | bytes 7077896 | tf_op jit(solution)/shard_map/ppermute | solution.py:21
  85.2 35.4 %copy-start = (f32[4,36864]{1,0:T(4,128)S(1)}, f32[4,36864]{1,0:T(4,128)}, u32[]{:S(2)}) copy-start(f32[4,36864]{1,0:T(4,128)} %param.12) | copy-start | bytes 1769476
  85.2 35.4 %copy-start.1 = (f32[4,36864]{1,0:T(4,128)S(1)}, f32[4,36864]{1,0:T(4,128)}, u32[]{:S(2)}) copy-start(f32[4,36864]{1,0:T(4,128)} %param.13) | copy-start | bytes 1769476
  85.2 70.3 %collective-permute-start.1 = (bf16[8,4,1,36864]{3,0,2,1:T(8,128)(2,1)}, bf16[8,4,1,36864]{3,0,2,1:T(8,128)(2,1)}, u32[]{:S(2)}, u32[]{:S(2)}) collective-permute-start(bf16[8,4,1,36864]{3,0,2,1:T(8,128)(2,1)} %copy.11), channel_id=1, source_target_pairs={{1,0},{2,1},{3,2},{4,3},{5,4},{6,5},{7,6},{8,7},{9,8},{10,9},{11,1... | collective-permute-start | bytes 7077896 | tf_op jit(solution)/shard_map/ppermute | solution.py:22
Sparse Core Ops, SparseCore 0:
  61.3 57.8 all-reduce.1
where the time goes:
time: 343 us; the launch traced here: 342 us
  other arithmetic  179 us (52%)
  local copies, waits for them, and re-layouts  89 us (26%)
  waiting for transfers between devices  51 us (15%)
  between operations  13.5 us (4%)
  starting transfers between devices  9.14 us (3%)
    dynamic_update_slice x8, other arithmetic, apply_bands(): return lax.map(one_band, padded_bands)  78.7 us
    psum x1, waiting for transfers between devices, shards(): summed = lax.psum(density.astype(jnp.bfloat16), 'ka').astype(jnp.float32)  28.3 us
    ppermute x1, waiting for transfers between devices, with_halo(): before = lax.ppermute(last, axis, up)  22.7 us
    add x8, other arithmetic, step_band(): return (carry + density_terms(band, weight), None)  22.6 us
    concatenate x1, other arithmetic, with_halo(): x = jnp.concatenate([before, x, after], axis=dim)  20.7 us
    convert_element_type x8, other arithmetic, apply_hamiltonian(): values = padded_band.astype(jnp.float32)  15.8 us
    slice x16, local copies, waits for them, and re-layouts, plane_neighbours(): jnp.roll(center, -1, -1)  15.2 us
    slice x16, local copies, waits for them, and re-layouts, plane_neighbours(): jnp.roll(center, row_length, -1) + jnp.roll(center, -row_length, -1)  15.2 us
  transfers between devices with their start and end apart: 3, of which 2 were waited for; matrix products, arithmetic and copies ran while one was open for 10% of the time, Pallas kernels for 0%

commit v1 on v0

v1 whole, which is shorter than its diff:
```python
import functools
import math

import jax
import jax.numpy as jnp
from jax import lax
from jax.experimental import pallas as pl
from jax.experimental.pallas import tpu as pltpu
from jax.sharding import PartitionSpec as P

NY = 192
FLOOR_FRACTION = 0.05
MESH = pl.DeviceIdType.MESH
LANES = 128
ROWS_PER_STEP = 16
LAST_PIECES = 4
DENSITY_PIECES = 4
EARLY = 2


def cube_root(x):
    root = jnp.exp(jnp.log(jnp.abs(x)) * (1.0 / 3.0))
    return jnp.where(x == 0.0, 0.0, jnp.where(x < 0.0, -root, root))


def halo_kernel(
    bands,
    tiles,
    kpt_ref,
    occ_ref,
    x_hbm,
    core_ref,
    local_ref,
    out_ref,
    xb,
    send_up,
    send_down,
    from_below,
    from_above,
    partial_,
    stage,
    stencil,
    own_density,
    partner_half,
    chip_half,
    opposite_half,
    relay,
    total_density,
    potential,
    load_sem,
    wrap_sem,
    up_send,
    up_recv,
    down_send,
    down_recv,
    pair_send,
    pair_recv,
    cross_send,
    cross_recv,
    relay_recv,
    relay_send,
    gather_send,
    gather_recv,
):
    ka, brick = lax.axis_index("ka"), lax.axis_index("brick")
    bricks = lax.axis_size("brick")
    groups = lax.axis_size("ka")
    side = lax.rem(ka, 2)
    has_above, has_below = brick < bricks - 1, brick > 0
    above = (ka, jnp.minimum(brick + 1, bricks - 1))
    below = (ka, jnp.maximum(brick - 1, 0))
    partner = (ka + 1 - 2 * side, brick)
    far = lax.rem(ka + 2, groups)
    opposite = (far, brick)
    mate = brick + 1 - 2 * lax.rem(brick, 2)
    row = lax.rem(brick, 4)
    edge = jnp.logical_or(row == 0, row == 3)
    inner = jnp.logical_not(edge)
    half = tiles // 2
    piece = half // DENSITY_PIECES
    direct = DENSITY_PIECES // 2

    barrier = pltpu.get_barrier_semaphore()

    @pl.when(has_above)
    def _():
        pl.semaphore_signal(barrier, inc=1, device_id=above, device_id_type=MESH)

    @pl.when(has_below)
    def _():
        pl.semaphore_signal(barrier, inc=1, device_id=below, device_id_type=MESH)

    for other in (partner, opposite, (far, mate)):
        pl.semaphore_signal(barrier, inc=1, device_id=other, device_id_type=MESH)

    def load(b, c):
        return pltpu.make_async_copy(
            x_hbm.at[b, c], xb.at[b, pl.ds(2, tiles), c], load_sem.at[b, c]
        )

    def wrap(end, c):
        source = tiles - 2 if end == 0 else 0
        target = 0 if end == 0 else tiles + 2
        return pltpu.make_async_copy(
            x_hbm.at[:, c, pl.ds(source, 2)],
            xb.at[:, pl.ds(target, 2), c],
            wrap_sem.at[end, c],
        )

    for b in range(bands):
        for c in range(4):
            load(b, c).start()
    for end in range(2):
        for c in range(4):
            wrap(end, c).start()

    last = bands - 1
    rows = 4 * tiles
    last_rows = rows // LAST_PIECES

    def slots(b):
        if b < last:
            return [(b, pl.ds(0, rows), b)]
        return [(b, pl.ds(k * last_rows, last_rows), last + k) for k in range(LAST_PIECES)]

    def up_copy(slot):
        b, r, s = slot
        return pltpu.make_async_remote_copy(
            send_up.at[b, r], from_below.at[b, r], up_send.at[s], up_recv.at[s],
            device_id=above, device_id_type=MESH,
        )

    def down_copy(slot):
        b, r, s = slot
        return pltpu.make_async_remote_copy(
            send_down.at[b, r], from_above.at[b, r], down_send.at[s], down_recv.at[s],
            device_id=below, device_id_type=MESH,
        )

    def extract(b):
        for c in range(4):
            load(b, c).wait()
        n = ROWS_PER_STEP

        def step(i, carry):
            j = i * n
            values = xb[b, pl.ds(2 + j, n)].reshape(n * 16, LANES)
            stage[...] = values.astype(jnp.float32)
            r = pl.multiple_of(4 * j, 4 * n)
            send_up[b, pl.ds(r, 4 * n)] = stage[pl.ds(3, 4 * n, stride=4)].astype(jnp.bfloat16)
            send_down[b, pl.ds(r, 4 * n)] = stage[pl.ds(0, 4 * n, stride=4)].astype(jnp.bfloat16)
            return carry

        lax.fori_loop(0, tiles // n, step, 0)

    def send(b):
        for slot in slots(b):

            @pl.when(has_above)
            def _():
                up_copy(slot).start()

            @pl.when(has_below)
            def _():
                down_copy(slot).start()

    for b in range(EARLY + 1):
        extract(b)
    pl.semaphore_wait(
        barrier, 3 + has_above.astype(jnp.int32) + has_below.astype(jnp.int32)
    )
    for b in range(EARLY):
        send(b)
    for b in range(EARLY + 1, bands):
        extract(b)

    low = lax.broadcasted_iota(jnp.int32, (8, LANES), 0) < 4
    weights = [
        (kpt_ref[b] * occ_ref[b]).astype(jnp.float32) * (1.0 / (2.0 * bands * groups))
        for b in range(bands)
    ]

    def swap(v):
        return pltpu.roll(v, 4, 0)

    def density_step(j, carry):
        for q in range(2):
            jj = 2 * j + q
            a = bb = cc = dd = None
            for b in range(bands):
                t = xb[b, 2 + jj].reshape(16, LANES).astype(jnp.float32)
                u, w = t[:8], t[8:]
                uw, ww = u * weights[b], w * weights[b]
                terms = (uw * u, ww * w, uw * w, uw * swap(w))
                if b == 0:
                    a, bb, cc, dd = terms
                else:
                    a, bb, cc, dd = (x + y for x, y in zip((a, bb, cc, dd), terms))
            n, z = a + bb, a - bb
            dd = jnp.where(low, dd, -dd)
            n, z = n + swap(n), z + swap(z)
            mx, my = 2.0 * (cc + swap(cc)), 2.0 * (dd + swap(dd))
            first = jnp.where(low, n, mx)
            second = jnp.where(low, my, z)
            own_density[jj] = jnp.concatenate([first, second], axis=0).astype(jnp.bfloat16)
        return carry

    mine, theirs = half * side, half * (1 - side)
    lax.fori_loop(
        0, half // 2, lambda i, c: density_step(theirs // 2 + i, c), 0
    )
    pair = pltpu.make_async_remote_copy(
        own_density.at[pl.ds(theirs, half)], partner_half, pair_send, pair_recv,
        device_id=partner, device_id_type=MESH,
    )
    lax.fori_loop(0, half // 2, lambda i, c: density_step(mine // 2 + i, c), 0)
    pair.start()

    def weights_of(t):
        i = lax.broadcasted_iota(jnp.int32, (6 * LANES, 2 * LANES), 0) + 2 * LANES * (t - 1)
        o = lax.broadcasted_iota(jnp.int32, (6 * LANES, 2 * LANES), 1) + 2 * LANES * t
        diff = i - o
        y = o - jnp.where(o >= NY, NY, 0) - jnp.where(o >= 2 * NY, NY, 0) - jnp.where(o >= 3 * NY, NY, 0)
        forward = jnp.where(y == NY - 1, 1 - NY, 1)
        backward = jnp.where(y == 0, NY - 1, -1)
        near = jnp.where(diff == forward, -0.5, 0.0) + jnp.where(diff == backward, -0.5, 0.0)
        across = jnp.where(diff == NY, -0.5, 0.0) + jnp.where(diff == -NY, -0.5, 0.0)
        return (near + across + jnp.where(diff == 0, 3.0, 0.0)).astype(jnp.bfloat16)

    for t in range(3):
        stencil[t] = weights_of(t)

    pair.wait()

    def cross_copy(k):
        return pltpu.make_async_remote_copy(
            chip_half.at[pl.ds(k * piece, piece)], opposite_half.at[pl.ds(k * piece, piece)],
            cross_send.at[k], cross_recv.at[k], device_id=opposite, device_id_type=MESH,
        )

    def first_leg(k):
        return pltpu.make_async_remote_copy(
            chip_half.at[pl.ds(k * piece, piece)], relay.at[k - direct],
            cross_send.at[k], relay_recv.at[k - direct],
            device_id=(ka, mate), device_id_type=MESH,
        )

    def second_leg(k):
        return pltpu.make_async_remote_copy(
            relay.at[k - direct], opposite_half.at[pl.ds(k * piece, piece)],
            relay_send.at[k - direct], cross_recv.at[k],
            device_id=(far, mate), device_id_type=MESH,
        )

    def sum_half(i, carry):
        a = own_density[mine + i].astype(jnp.float32)
        chip_half[i] = (a + partner_half[i].astype(jnp.float32)).astype(jnp.bfloat16)
        return carry

    def cross_start(k):
        if k < direct:
            cross_copy(k).start()
        else:

            @pl.when(edge)
            def _():
                first_leg(k).start()

            @pl.when(inner)
            def _():
                cross_copy(k).start()

    order = list(range(direct, DENSITY_PIECES)) + list(range(direct))
    for n, k in enumerate(order):
        lax.fori_loop(k * piece, (k + 1) * piece, sum_half, 0)
        if n:
            cross_start(order[n - 1])
    send(EARLY)
    cross_start(order[-1])
    for b in range(EARLY + 1, bands):
        send(b)

    for end in range(2):
        for c in range(4):
            wrap(end, c).wait()

    @pl.when(jnp.logical_not(has_below))
    def _():
        from_below[...] = jnp.zeros_like(from_below)

    @pl.when(jnp.logical_not(has_above))
    def _():
        from_above[...] = jnp.zeros_like(from_above)

    for k in range(direct, DENSITY_PIECES):

        @pl.when(inner)
        def _():
            first_leg(k).wait_recv()
            second_leg(k).start()

    def sum_total(i, carry):
        a = chip_half[i].astype(jnp.float32)
        total_density[mine + i] = (a + opposite_half[i].astype(jnp.float32)).astype(jnp.bfloat16)
        return carry

    def gather(k):
        r = pl.ds(mine + k * piece, piece)
        return pltpu.make_async_remote_copy(
            total_density.at[r], total_density.at[r], gather_send.at[k], gather_recv.at[k],
            device_id=partner, device_id_type=MESH,
        )

    order = list(range(DENSITY_PIECES))
    for k in order:
        cross_copy(k).wait_recv()
        lax.fori_loop(k * piece, (k + 1) * piece, sum_total, 0)
        if k:
            gather(k - 1).start()

    def potential_step(j, carry):
        t = total_density[j].astype(jnp.float32)
        first, second = t[:8], t[8:]
        other_first, other_second = swap(first), swap(second)
        n = jnp.where(low, first, other_first)
        mx = jnp.where(low, other_first, first)
        my = jnp.where(low, second, other_second)
        z = jnp.where(low, other_second, second)
        core = core_ref[j]
        local = local_ref[j]
        electrons = n + jnp.concatenate([core, core], axis=0)
        magnitude = jnp.sqrt(mx * mx + my * my + z * z)
        upper = -cube_root(3.0 / math.pi * (electrons + magnitude))
        lower = -cube_root(3.0 / math.pi * (electrons - magnitude))
        factor = 0.5 * (upper - lower) / jnp.maximum(magnitude, FLOOR_FRACTION * electrons)
        v = 0.5 * (upper + lower) + jnp.concatenate([local, local], axis=0)
        bz, by = factor * z, factor * my
        potential[j, 0] = v + bz
        potential[j, 1] = v - bz
        potential[j, 2] = factor * mx
        potential[j, 3] = jnp.where(low, by, -by)
        return carry

    lax.fori_loop(mine, mine + (DENSITY_PIECES - 1) * piece, potential_step, 0)
    gather(DENSITY_PIECES - 1).start()
    lax.fori_loop(mine + (DENSITY_PIECES - 1) * piece, mine + half, potential_step, 0)

    def gathered(k):
        r = pl.ds(theirs + k * piece, piece)
        return pltpu.make_async_remote_copy(
            total_density.at[r], total_density.at[r], gather_send.at[k], gather_recv.at[k],
            device_id=partner, device_id_type=MESH,
        )

    for k in range(DENSITY_PIECES):
        gathered(k).wait_recv()
        lax.fori_loop(theirs + k * piece, theirs + (k + 1) * piece, potential_step, 0)

    plane = lax.rem(lax.broadcasted_iota(jnp.int32, (8, LANES), 0), 4)
    lower_edge, upper_edge = plane == 0, plane == 3

    def normal(v):
        down = jnp.where(lower_edge, 0.0, pltpu.roll(v, 1, 0))
        up = jnp.where(upper_edge, 0.0, pltpu.roll(v, 7, 0))
        return -0.5 * (down + up)

    group = 8

    def apply(b, target):
        def step(i, carry):
            j0 = i * (6 * group)
            values = xb[b, pl.ds(j0, 6 * group + 4)].reshape(6 * group + 4, 16, LANES)
            for t in range(3):
                left = jnp.concatenate(
                    [
                        jnp.concatenate(
                            [values[6 * g + 2 * t + q] for g in range(group)], axis=0
                        )
                        for q in range(6)
                    ],
                    axis=1,
                )
                product = jnp.dot(left, stencil[t], preferred_element_type=jnp.float32)
                for g in range(group):
                    for e in range(2):
                        k = 6 * g + 2 * t + e
                        j = j0 + k
                        x = values[k + 2].astype(jnp.float32)
                        u, w = x[:8], x[8:]
                        r = product[16 * g : 16 * g + 16, LANES * e : LANES * (e + 1)]
                        bx, by = potential[j, 2], potential[j, 3]
                        hu = r[:8] + normal(u) + potential[j, 0] * u + bx * w + by * swap(w)
                        hw = r[8:] + normal(w) + potential[j, 1] * w + bx * u - by * swap(u)
                        s = pl.multiple_of(16 * j, 16)
                        partial_[target, pl.ds(s, 8)] = hu
                        partial_[target, pl.ds(s + 8, 8)] = hw
            return carry

        lax.fori_loop(0, tiles // (6 * group), step, 0)

    def finish(b, source):
        n = ROWS_PER_STEP

        def step(i, carry):
            r = pl.multiple_of(4 * n * i, 4 * n)
            s = pl.multiple_of(16 * n * i, 16 * n)
            below_values = from_below[b, pl.ds(r, 4 * n)].astype(jnp.float32)
            above_values = from_above[b, pl.ds(r, 4 * n)].astype(jnp.float32)
            lows, highs = pl.ds(s, 4 * n, stride=4), pl.ds(s + 3, 4 * n, stride=4)
            view = partial_.at[source]
            view[lows] = view[lows] - 0.5 * below_values
            view[highs] = view[highs] - 0.5 * above_values
            done = view[pl.ds(s, 16 * n)].astype(jnp.bfloat16)
            out_ref[b, pl.ds(n * i, n)] = done.reshape(n, 4, 4, LANES)
            return carry

        per_slot = tiles // n // len(slots(b))
        rest = tiles // n - per_slot * len(slots(b))
        start = 0
        for m, slot in enumerate(slots(b)):

            @pl.when(has_below)
            def _():
                up_copy(slot).wait_recv()

            @pl.when(has_above)
            def _():
                down_copy(slot).wait_recv()

            stop = ((m + 1) * tiles // len(slots(b))) // n
            lax.fori_loop(start, stop, step, 0)
            start = stop

    apply(0, 0)
    for b in range(1, bands):
        apply(b, b % 2)
        finish(b - 1, (b - 1) % 2)

    pair_done = []
    for k in range(DENSITY_PIECES):
        cross_copy(k).wait_send()
        gather(k).wait_send()
    for k in range(direct, DENSITY_PIECES):

        @pl.when(inner)
        def _():
            second_leg(k).wait_send()

    for b in range(bands):
        for slot in slots(b):

            @pl.when(has_above)
            def _():
                up_copy(slot).wait_send()

            @pl.when(has_below)
            def _():
                down_copy(slot).wait_send()

    finish(last, last % 2)


def write_kernel(bands, in_ref, out_hbm, sem):
    copies = [
        pltpu.make_async_copy(in_ref.at[b, :, c], out_hbm.at[b, c], sem.at[b, c])
        for b in range(bands)
        for c in range(4)
    ]
    for copy in copies:
        copy.start()
    for copy in copies:
        copy.wait()


def shards(spinors, kpt_mult, occupied, core_density, local_potential):
    bands, parts, planes, cells = spinors.shape
    tiles = cells // LANES
    half = tiles // 2
    piece = half // DENSITY_PIECES
    relayed = DENSITY_PIECES - DENSITY_PIECES // 2
    copies = bands - 1 + LAST_PIECES
    bf16, f32 = jnp.bfloat16, jnp.float32
    view = spinors.reshape(bands, parts, planes, tiles, LANES).transpose(0, 1, 3, 2, 4)
    core = core_density.reshape(planes, tiles, LANES).transpose(1, 0, 2)
    local = local_potential.reshape(planes, tiles, LANES).transpose(1, 0, 2)
    dma = pltpu.SemaphoreType.DMA
    in_vmem = pl.BlockSpec(memory_space=pltpu.VMEM)
    in_smem = pl.BlockSpec(memory_space=pltpu.SMEM)
    anywhere = pl.BlockSpec(memory_space=pl.ANY)
    applied = pl.pallas_call(
        functools.partial(halo_kernel, bands, tiles),
        out_shape=pltpu.VMEM((bands, tiles, parts, planes, LANES), bf16),
        in_specs=[in_smem, in_smem, anywhere, in_vmem, in_vmem],
        out_specs=in_vmem,
        scratch_shapes=[
            pltpu.VMEM((bands, tiles + 4, parts, planes, LANES), bf16),
            pltpu.VMEM((bands, 4 * tiles, LANES), bf16),
            pltpu.VMEM((bands, 4 * tiles, LANES), bf16),
            pltpu.VMEM((bands, 4 * tiles, LANES), bf16),
            pltpu.VMEM((bands, 4 * tiles, LANES), bf16),
            pltpu.VMEM((2, 16 * tiles, LANES), f32),
            pltpu.VMEM((16 * ROWS_PER_STEP, LANES), f32),
            pltpu.VMEM((3, 6 * LANES, 2 * LANES), bf16),
            pltpu.VMEM((tiles, 16, LANES), bf16),
            pltpu.VMEM((half, 16, LANES), bf16),
            pltpu.VMEM((half, 16, LANES), bf16),
            pltpu.VMEM((half, 16, LANES), bf16),
            pltpu.VMEM((relayed, piece, 16, LANES), bf16),
            pltpu.VMEM((tiles, 16, LANES), bf16),
            pltpu.VMEM((tiles, 4, 8, LANES), f32),
            dma((bands, 4)),
            dma((2, 4)),
            dma((copies,)),
            dma((copies,)),
            dma((copies,)),
            dma((copies,)),
            dma,
            dma,
            dma((DENSITY_PIECES,)),
            dma((DENSITY_PIECES,)),
            dma((relayed,)),
            dma((relayed,)),
            dma((DENSITY_PIECES,)),
            dma((DENSITY_PIECES,)),
        ],
        compiler_params=pltpu.CompilerParams(
            collective_id=0, has_side_effects=True, vmem_limit_bytes=48 << 20
        ),
    )(kpt_mult, occupied, view, core, local)
    written = pl.pallas_call(
        functools.partial(write_kernel, bands),
        out_shape=jax.ShapeDtypeStruct((bands, parts, tiles, planes, LANES), bf16),
        in_specs=[in_vmem],
        out_specs=anywhere,
        scratch_shapes=[dma((bands, 4))],
        compiler_params=pltpu.CompilerParams(vmem_limit_bytes=4 << 20),
    )(pltpu.with_memory_space_constraint(applied, pltpu.VMEM))
    return written.transpose(0, 1, 3, 2, 4).reshape(bands, parts, planes, cells)


def solution(mesh):
    placed = (P("ka", None, "brick", None), P("ka"), P("ka"), P("brick", None), P("brick", None))
    return jax.shard_map(
        shards, mesh=mesh, in_specs=placed, out_specs=P("ka", None, "brick", None), check_vma=False
    )
```

time: 343 us -> 84.6 us (0.25)
  other arithmetic: 179 us -> 0 us
  local copies, waits for them, and re-layouts: 89 us -> 0 us
  Pallas kernels: 0 us -> 83.8 us
  waiting for transfers between devices: 51 us -> 0 us
  between operations: 13.5 us -> 0.01 us
  starting transfers between devices: 9.14 us -> 0 us
    pallas_call x0 -> x2, Pallas kernels: none -> 83.8 us  [the longest x1 80 us: shards(): pl.pallas_call(functools.partial(halo_kernel, bands, tiles), out_shape=pl...]
    dynamic_update_slice x8 -> x0, other arithmetic: 78.7 us -> none  [apply_bands(): return lax.map(one_band, padded_bands)]
    slice x49 -> x0, local copies, waits for them, and re-layouts: 58 us -> none  [the longest x16 15.2 us: plane_neighbours(): jnp.roll(center, -1, -1)]
    add x24 -> x0, other arithmetic: 44.2 us -> none  [the longest x8 22.6 us: step_band(): return (carry + density_terms(band, weight), None)]
    convert_element_type x18 -> x0, other arithmetic: 30.1 us -> none  [the longest x8 15.8 us: apply_hamiltonian(): values = padded_band.astype(jnp.float32)]
    psum x1 -> x0, waiting for transfers between devices: 28.3 us -> none  [shards(): summed = lax.psum(density.astype(jnp.bfloat16), 'ka').astype(jnp.float32)]
    ppermute x2 -> x0, waiting for transfers between devices: 22.7 us -> none  [the longest x1 22.7 us: with_halo(): before = lax.ppermute(last, axis, up)]
    concatenate x1 -> x0, other arithmetic: 20.7 us -> none  [with_halo(): x = jnp.concatenate([before, x, after], axis=dim)]
  transfers between devices with their start and end apart: 3 -> 0, of which waited for: 2 -> 0; matrix products, arithmetic and copies ran while one was open for 10% -> 0% of each run, Pallas kernels for 0% -> 0%
where the time goes in v1:
time: 84.6 us; the launch traced here: 83.8 us
  Pallas kernels  83.8 us (99%)
    pallas_call x1, Pallas kernels, shards(): pl.pallas_call(functools.partial(halo_kernel, bands, tiles), out_shape=pl...  80 us
    pallas_call x1, Pallas kernels, shards(): pl.pallas_call(functools.partial(write_kernel, bands), out_shape=jax.Shap...  3.87 us

profile of v1, /device:TPU:96, one launch (start us, length us, event | category | flops | bytes accessed | tf_op | source)
XLA Modules:
  0.0 83.8 jit_solution(7080642664652729442)
XLA Ops:
  0.0 80.0 %shard_map.55.in_ref = bf16[8,288,4,4,128]{4,3,2,1,0:T(4,128)(2,1)S(1)} custom-call(s32[8]{0:T(128)} %kpt_ref.1, s32[8]{0:T(128)} %occ_ref.1, bf16[8,4,288,4,128]{4,3,2,1,0:T(4,128)(2,1)} %bitcast.12, f32[288,4,128]{2,1,0:T(4,128)} %bitcast.13, f32[288,4,128]{2,1,0:T(4,128)} %bitcast.14), custom_call_target="tpu_custom_call" | custom-call | tf_op jit(solution)/shard_map/pallas_call | solution.py:490
  80.0 3.9 %shard_map.56 = bf16[8,4,288,4,128]{4,3,2,1,0:T(4,128)(2,1)} custom-call(bf16[8,288,4,4,128]{4,3,2,1,0:T(4,128)(2,1)S(1)} %shard_map.55.in_ref), custom_call_target="tpu_custom_call" | custom-call | tf_op jit(solution)/shard_map/pallas_call | solution.py:530

commit v2 on v1

--- a/solution.py
+++ b/solution.py
@@ -15,6 +15,9 @@
 ROWS_PER_STEP = 16
 LAST_PIECES = 4
 DENSITY_PIECES = 4
+MIX_STEP = 8
+SUM_STEP = 6
+POTENTIAL_STEP = 6
 EARLY = 2
 
 
@@ -40,6 +43,7 @@
     partial_,
     stage,
     stencil,
+    normal,
     own_density,
     partner_half,
     chip_half,
@@ -95,7 +99,7 @@
 
     def load(b, c):
         return pltpu.make_async_copy(
-            x_hbm.at[b, c], xb.at[b, pl.ds(2, tiles), c], load_sem.at[b, c]
+            x_hbm.at[b, c], xb.at[b, pl.ds(2, tiles), pl.ds(4 * c, 4)], load_sem.at[b, c]
         )
 
     def wrap(end, c):
@@ -103,7 +107,7 @@
         target = 0 if end == 0 else tiles + 2
         return pltpu.make_async_copy(
             x_hbm.at[:, c, pl.ds(source, 2)],
-            xb.at[:, pl.ds(target, 2), c],
+            xb.at[:, pl.ds(target, 2), pl.ds(4 * c, 4)],
             wrap_sem.at[end, c],
         )
 
@@ -164,15 +168,35 @@
             def _():
                 down_copy(slot).start()
 
-    for b in range(EARLY + 1):
+    for b in range(bands):
         extract(b)
+
+    def weights_of(t):
+        i = lax.broadcasted_iota(jnp.int32, (6 * LANES, 2 * LANES), 0) + 2 * LANES * (t - 1)
+        o = lax.broadcasted_iota(jnp.int32, (6 * LANES, 2 * LANES), 1) + 2 * LANES * t
+        diff = i - o
+        y = o - jnp.where(o >= NY, NY, 0) - jnp.where(o >= 2 * NY, NY, 0) - jnp.where(o >= 3 * NY, NY, 0)
+        forward = jnp.where(y == NY - 1, 1 - NY, 1)
+        backward = jnp.where(y == 0, NY - 1, -1)
+        near = jnp.where(diff == forward, -0.5, 0.0) + jnp.where(diff == backward, -0.5, 0.0)
+        across = jnp.where(diff == NY, -0.5, 0.0) + jnp.where(diff == -NY, -0.5, 0.0)
+        return (near + across + jnp.where(diff == 0, 3.0, 0.0)).astype(jnp.bfloat16)
+
+    for t in range(3):
+        stencil[t] = weights_of(t)
+    size = LANES
+    p = lax.broadcasted_iota(jnp.int32, (size, size), 0)
+    q = lax.broadcasted_iota(jnp.int32, (size, size), 1)
+    plane = lax.rem(p, 4)
+    under = jnp.where(plane == 0, 0.0, jnp.where(p - q == 1, -0.5, 0.0))
+    over = jnp.where(plane == 3, 0.0, jnp.where(q - p == 1, -0.5, 0.0))
+    normal[...] = (under + over).astype(jnp.bfloat16)
+
     pl.semaphore_wait(
         barrier, 3 + has_above.astype(jnp.int32) + has_below.astype(jnp.int32)
     )
     for b in range(EARLY):
         send(b)
-    for b in range(EARLY + 1, bands):
-        extract(b)
 
     low = lax.broadcasted_iota(jnp.int32, (8, LANES), 0) < 4
     weights = [
@@ -188,7 +212,7 @@
             jj = 2 * j + q
             a = bb = cc = dd = None
             for b in range(bands):
-                t = xb[b, 2 + jj].reshape(16, LANES).astype(jnp.float32)
+                t = xb[b, 2 + jj].astype(jnp.float32)
                 u, w = t[:8], t[8:]
                 uw, ww = u * weights[b], w * weights[b]
                 terms = (uw * u, ww * w, uw * w, uw * swap(w))
@@ -213,22 +237,9 @@
         own_density.at[pl.ds(theirs, half)], partner_half, pair_send, pair_recv,
         device_id=partner, device_id_type=MESH,
     )
-    lax.fori_loop(0, half // 2, lambda i, c: density_step(mine // 2 + i, c), 0)
+    lax.fori_loop(0, half // 16, lambda i, c: density_step(mine // 2 + i, c), 0)
     pair.start()
-
-    def weights_of(t):
-        i = lax.broadcasted_iota(jnp.int32, (6 * LANES, 2 * LANES), 0) + 2 * LANES * (t - 1)
-        o = lax.broadcasted_iota(jnp.int32, (6 * LANES, 2 * LANES), 1) + 2 * LANES * t
-        diff = i - o
-        y = o - jnp.where(o >= NY, NY, 0) - jnp.where(o >= 2 * NY, NY, 0) - jnp.where(o >= 3 * NY, NY, 0)
-        forward = jnp.where(y == NY - 1, 1 - NY, 1)
-        backward = jnp.where(y == 0, NY - 1, -1)
-        near = jnp.where(diff == forward, -0.5, 0.0) + jnp.where(diff == backward, -0.5, 0.0)
-        across = jnp.where(diff == NY, -0.5, 0.0) + jnp.where(diff == -NY, -0.5, 0.0)
-        return (near + across + jnp.where(diff == 0, 3.0, 0.0)).astype(jnp.bfloat16)
-
-    for t in range(3):
-        stencil[t] = weights_of(t)
+    lax.fori_loop(half // 16, half // 2, lambda i, c: density_step(mine // 2 + i, c), 0)
 
     pair.wait()
 
@@ -253,8 +264,9 @@
         )
 
     def sum_half(i, carry):
-        a = own_density[mine + i].astype(jnp.float32)
-        chip_half[i] = (a + partner_half[i].astype(jnp.float32)).astype(jnp.bfloat16)
+        r = pl.ds(SUM_STEP * i, SUM_STEP)
+        a = own_density[pl.ds(mine + SUM_STEP * i, SUM_STEP)].astype(jnp.float32)
+        chip_half[r] = (a + partner_half[r].astype(jnp.float32)).astype(jnp.bfloat16)
         return carry
 
     def cross_start(k):
@@ -272,7 +284,7 @@
 
     order = list(range(direct, DENSITY_PIECES)) + list(range(direct))
     for n, k in enumerate(order):
-        lax.fori_loop(k * piece, (k + 1) * piece, sum_half, 0)
+        lax.fori_loop(k * piece // SUM_STEP, (k + 1) * piece // SUM_STEP, sum_half, 0)
         if n:
             cross_start(order[n - 1])
     send(EARLY)
@@ -292,16 +304,56 @@
     def _():
         from_above[...] = jnp.zeros_like(from_above)
 
+    group = 8
+
+    def kinetic(b):
+        view = partial_.at[b]
+
+        def step(i, carry):
+            j0 = i * (6 * group)
+            values = xb[b, pl.ds(j0, 6 * group + 4)]
+
+            def block(first, count):
+                return jnp.concatenate(
+                    [
+                        jnp.concatenate([values[6 * g + first + q] for g in range(group)], axis=0)
+                        for q in range(count)
+                    ],
+                    axis=1,
+                )
+
+            for t in range(3):
+                product = jnp.dot(
+                    block(2 * t, 6), stencil[t], preferred_element_type=jnp.float32
+                ) + jnp.dot(
+                    normal[...], block(2 * t + 2, 2), preferred_element_type=jnp.float32
+                )
+                for g in range(group):
+                    for e in range(2):
+                        s = pl.multiple_of(16 * (j0 + 6 * g + 2 * t + e), 16)
+                        view[pl.ds(s, 16)] = product[
+                            16 * g : 16 * g + 16, LANES * e : LANES * (e + 1)
+                        ]
+            return carry
+
+        lax.fori_loop(0, tiles // (6 * group), step, 0)
+
+    kinetic(0)
     for k in range(direct, DENSITY_PIECES):
+        kinetic(k - direct + 1)
 
         @pl.when(inner)
         def _():
             first_leg(k).wait_recv()
             second_leg(k).start()
 
+    for b in range(DENSITY_PIECES - direct + 1, bands):
+        kinetic(b)
+
     def sum_total(i, carry):
-        a = chip_half[i].astype(jnp.float32)
-        total_density[mine + i] = (a + opposite_half[i].astype(jnp.float32)).astype(jnp.bfloat16)
+        r = pl.ds(SUM_STEP * i, SUM_STEP)
+        a = chip_half[r].astype(jnp.float32) + opposite_half[r].astype(jnp.float32)
+        total_density[pl.ds(mine + SUM_STEP * i, SUM_STEP)] = a.astype(jnp.bfloat16)
         return carry
 
     def gather(k):
@@ -314,11 +366,11 @@
     order = list(range(DENSITY_PIECES))
     for k in order:
         cross_copy(k).wait_recv()
-        lax.fori_loop(k * piece, (k + 1) * piece, sum_total, 0)
+        lax.fori_loop(k * piece // SUM_STEP, (k + 1) * piece // SUM_STEP, sum_total, 0)
         if k:
             gather(k - 1).start()
 
-    def potential_step(j, carry):
+    def potential_of(j):
         t = total_density[j].astype(jnp.float32)
         first, second = t[:8], t[8:]
         other_first, other_second = swap(first), swap(second)
@@ -339,11 +391,18 @@
         potential[j, 1] = v - bz
         potential[j, 2] = factor * mx
         potential[j, 3] = jnp.where(low, by, -by)
-        return carry
-
-    lax.fori_loop(mine, mine + (DENSITY_PIECES - 1) * piece, potential_step, 0)
+
+    def potential_range(start, count):
+        def step(i, carry):
+            for q in range(POTENTIAL_STEP):
+                potential_of(start + POTENTIAL_STEP * i + q)
+            return carry
+
+        lax.fori_loop(0, count // POTENTIAL_STEP, step, 0)
+
+    potential_range(mine, (DENSITY_PIECES - 1) * piece)
     gather(DENSITY_PIECES - 1).start()
-    lax.fori_loop(mine + (DENSITY_PIECES - 1) * piece, mine + half, potential_step, 0)
+    potential_range(mine + (DENSITY_PIECES - 1) * piece, piece)
 
     def gathered(k):
         r = pl.ds(theirs + k * piece, piece)
@@ -354,51 +413,27 @@
 
     for k in range(DENSITY_PIECES):
         gathered(k).wait_recv()
-        lax.fori_loop(theirs + k * piece, theirs + (k + 1) * piece, potential_step, 0)
-
-    plane = lax.rem(lax.broadcasted_iota(jnp.int32, (8, LANES), 0), 4)
-    lower_edge, upper_edge = plane == 0, plane == 3
-
-    def normal(v):
-        down = jnp.where(lower_edge, 0.0, pltpu.roll(v, 1, 0))
-        up = jnp.where(upper_edge, 0.0, pltpu.roll(v, 7, 0))
-        return -0.5 * (down + up)
-
-    group = 8
-
-    def apply(b, target):
+        potential_range(theirs + k * piece, piece)
+
+    def mix(b):
+        view = partial_.at[b]
+
         def step(i, carry):
-            j0 = i * (6 * group)
-            values = xb[b, pl.ds(j0, 6 * group + 4)].reshape(6 * group + 4, 16, LANES)
-            for t in range(3):
-                left = jnp.concatenate(
-                    [
-                        jnp.concatenate(
-                            [values[6 * g + 2 * t + q] for g in range(group)], axis=0
-                        )
-                        for q in range(6)
-                    ],
-                    axis=1,
-                )
-                product = jnp.dot(left, stencil[t], preferred_element_type=jnp.float32)
-                for g in range(group):
-                    for e in range(2):
-                        k = 6 * g + 2 * t + e
-                        j = j0 + k
-                        x = values[k + 2].astype(jnp.float32)
-                        u, w = x[:8], x[8:]
-                        r = product[16 * g : 16 * g + 16, LANES * e : LANES * (e + 1)]
-                        bx, by = potential[j, 2], potential[j, 3]
-                        hu = r[:8] + normal(u) + potential[j, 0] * u + bx * w + by * swap(w)
-                        hw = r[8:] + normal(w) + potential[j, 1] * w + bx * u - by * swap(u)
-                        s = pl.multiple_of(16 * j, 16)
-                        partial_[target, pl.ds(s, 8)] = hu
-                        partial_[target, pl.ds(s + 8, 8)] = hw
+            for q in range(MIX_STEP):
+                j = i * MIX_STEP + q
+                x = xb[b, j + 2].astype(jnp.float32)
+                u, w = x[:8], x[8:]
+                s = pl.multiple_of(16 * j, 16)
+                bx, by = potential[j, 2], potential[j, 3]
+                hu = view[pl.ds(s, 8)] + potential[j, 0] * u + bx * w + by * swap(w)
+                hw = view[pl.ds(s + 8, 8)] + potential[j, 1] * w + bx * u - by * swap(u)
+                view[pl.ds(s, 8)] = hu
+                view[pl.ds(s + 8, 8)] = hw
             return carry
 
-        lax.fori_loop(0, tiles // (6 * group), step, 0)
-
-    def finish(b, source):
+        lax.fori_loop(0, tiles // MIX_STEP, step, 0)
+
+    def finish(b):
         n = ROWS_PER_STEP
 
         def step(i, carry):
@@ -407,11 +442,11 @@
             below_values = from_below[b, pl.ds(r, 4 * n)].astype(jnp.float32)
             above_values = from_above[b, pl.ds(r, 4 * n)].astype(jnp.float32)
             lows, highs = pl.ds(s, 4 * n, stride=4), pl.ds(s + 3, 4 * n, stride=4)
-            view = partial_.at[source]
+            view = partial_.at[b]
             view[lows] = view[lows] - 0.5 * below_values
             view[highs] = view[highs] - 0.5 * above_values
             done = view[pl.ds(s, 16 * n)].astype(jnp.bfloat16)
-            out_ref[b, pl.ds(n * i, n)] = done.reshape(n, 4, 4, LANES)
+            out_ref[b, pl.ds(n * i, n)] = done.reshape(n, 16, LANES)
             return carry
 
         per_slot = tiles // n // len(slots(b))
@@ -431,10 +466,10 @@
             lax.fori_loop(start, stop, step, 0)
             start = stop
 
-    apply(0, 0)
-    for b in range(1, bands):
-        apply(b, b % 2)
-        finish(b - 1, (b - 1) % 2)
+    for b in range(bands):
+        mix(b)
+    for b in range(last):
+        finish(b)
 
     pair_done = []
     for k in range(DENSITY_PIECES):
@@ -457,12 +492,12 @@
             def _():
                 down_copy(slot).wait_send()
 
-    finish(last, last % 2)
+    finish(last)
 
 
 def write_kernel(bands, in_ref, out_hbm, sem):
     copies = [
-        pltpu.make_async_copy(in_ref.at[b, :, c], out_hbm.at[b, c], sem.at[b, c])
+        pltpu.make_async_copy(in_ref.at[b, :, pl.ds(4 * c, 4)], out_hbm.at[b, c], sem.at[b, c])
         for b in range(bands)
         for c in range(4)
     ]
@@ -489,18 +524,19 @@
     anywhere = pl.BlockSpec(memory_space=pl.ANY)
     applied = pl.pallas_call(
         functools.partial(halo_kernel, bands, tiles),
-        out_shape=pltpu.VMEM((bands, tiles, parts, planes, LANES), bf16),
+        out_shape=pltpu.VMEM((bands, tiles, parts * planes, LANES), bf16),
         in_specs=[in_smem, in_smem, anywhere, in_vmem, in_vmem],
         out_specs=in_vmem,
         scratch_shapes=[
-            pltpu.VMEM((bands, tiles + 4, parts, planes, LANES), bf16),
+            pltpu.VMEM((bands, tiles + 4, parts * planes, LANES), bf16),
             pltpu.VMEM((bands, 4 * tiles, LANES), bf16),
             pltpu.VMEM((bands, 4 * tiles, LANES), bf16),
             pltpu.VMEM((bands, 4 * tiles, LANES), bf16),
             pltpu.VMEM((bands, 4 * tiles, LANES), bf16),
-            pltpu.VMEM((2, 16 * tiles, LANES), f32),
+            pltpu.VMEM((bands, 16 * tiles, LANES), f32),
             pltpu.VMEM((16 * ROWS_PER_STEP, LANES), f32),
             pltpu.VMEM((3, 6 * LANES, 2 * LANES), bf16),
+            pltpu.VMEM((LANES, LANES), bf16),
             pltpu.VMEM((tiles, 16, LANES), bf16),
             pltpu.VMEM((half, 16, LANES), bf16),
             pltpu.VMEM((half, 16, LANES), bf16),
@@ -524,7 +560,7 @@
             dma((DENSITY_PIECES,)),
         ],
         compiler_params=pltpu.CompilerParams(
-            collective_id=0, has_side_effects=True, vmem_limit_bytes=48 << 20
+            collective_id=0, has_side_effects=True, vmem_limit_bytes=54 << 20
         ),
     )(kpt_mult, occupied, view, core, local)
     written = pl.pallas_call(

time: 84.6 us -> 72.4 us (0.86)
  Pallas kernels: 83.8 us -> 72.2 us
    pallas_call x1, Pallas kernels: 80 us -> 68.4 us  [shards(): pl.pallas_call(functools.partial(halo_kernel, bands, tiles), out_shape=pl...]
where the time goes in v2:
time: 72.4 us; the launch traced here: 72.2 us
  Pallas kernels  72.2 us (100%)
    pallas_call x1, Pallas kernels, shards(): pl.pallas_call(functools.partial(halo_kernel, bands, tiles), out_shape=pl...  68.4 us
    pallas_call x1, Pallas kernels, shards(): pl.pallas_call(functools.partial(write_kernel, bands), out_shape=jax.Shap...  3.87 us

profile of v2, /device:TPU:96, one launch (start us, length us, event | category | flops | bytes accessed | tf_op | source)
XLA Modules:
  0.0 72.2 jit_solution(14820341087838176632)
XLA Ops:
  0.0 68.4 %shard_map.55.in_ref = bf16[8,288,16,128]{3,2,1,0:T(8,128)(2,1)S(1)} custom-call(s32[8]{0:T(128)} %kpt_ref.1, s32[8]{0:T(128)} %occ_ref.1, bf16[8,4,288,4,128]{4,3,2,1,0:T(4,128)(2,1)} %bitcast.12, f32[288,4,128]{2,1,0:T(4,128)} %bitcast.13, f32[288,4,128]{2,1,0:T(4,128)} %bitcast.14), custom_call_target="tpu_custom_call" | custom-call | tf_op jit(solution)/shard_map/pallas_call | solution.py:525
  68.4 3.9 %shard_map.56 = bf16[8,4,288,4,128]{4,3,2,1,0:T(4,128)(2,1)} custom-call(bf16[8,288,16,128]{3,2,1,0:T(8,128)(2,1)S(1)} %shard_map.55.in_ref), custom_call_target="tpu_custom_call" | custom-call | tf_op jit(solution)/shard_map/pallas_call | solution.py:566

commit v3 on v2

--- a/solution.py
+++ b/solution.py
@@ -29,12 +29,16 @@
 def halo_kernel(
     bands,
     tiles,
+    kpt_hbm,
+    occ_hbm,
+    x_hbm,
+    core_hbm,
+    local_hbm,
+    out_ref,
     kpt_ref,
     occ_ref,
-    x_hbm,
     core_ref,
     local_ref,
-    out_ref,
     xb,
     send_up,
     send_down,
@@ -53,6 +57,7 @@
     potential,
     load_sem,
     wrap_sem,
+    field_sem,
     up_send,
     up_recv,
     down_send,
@@ -117,59 +122,14 @@
     for end in range(2):
         for c in range(4):
             wrap(end, c).start()
-
-    last = bands - 1
-    rows = 4 * tiles
-    last_rows = rows // LAST_PIECES
-
-    def slots(b):
-        if b < last:
-            return [(b, pl.ds(0, rows), b)]
-        return [(b, pl.ds(k * last_rows, last_rows), last + k) for k in range(LAST_PIECES)]
-
-    def up_copy(slot):
-        b, r, s = slot
-        return pltpu.make_async_remote_copy(
-            send_up.at[b, r], from_below.at[b, r], up_send.at[s], up_recv.at[s],
-            device_id=above, device_id_type=MESH,
-        )
-
-    def down_copy(slot):
-        b, r, s = slot
-        return pltpu.make_async_remote_copy(
-            send_down.at[b, r], from_above.at[b, r], down_send.at[s], down_recv.at[s],
-            device_id=below, device_id_type=MESH,
-        )
-
-    def extract(b):
-        for c in range(4):
-            load(b, c).wait()
-        n = ROWS_PER_STEP
-
-        def step(i, carry):
-            j = i * n
-            values = xb[b, pl.ds(2 + j, n)].reshape(n * 16, LANES)
-            stage[...] = values.astype(jnp.float32)
-            r = pl.multiple_of(4 * j, 4 * n)
-            send_up[b, pl.ds(r, 4 * n)] = stage[pl.ds(3, 4 * n, stride=4)].astype(jnp.bfloat16)
-            send_down[b, pl.ds(r, 4 * n)] = stage[pl.ds(0, 4 * n, stride=4)].astype(jnp.bfloat16)
-            return carry
-
-        lax.fori_loop(0, tiles // n, step, 0)
-
-    def send(b):
-        for slot in slots(b):
-
-            @pl.when(has_above)
-            def _():
-                up_copy(slot).start()
-
-            @pl.when(has_below)
-            def _():
-                down_copy(slot).start()
-
-    for b in range(bands):
-        extract(b)
+    fields = [
+        pltpu.make_async_copy(source, target, field_sem.at[k])
+        for k, (source, target) in enumerate(
+            ((kpt_hbm, kpt_ref), (occ_hbm, occ_ref), (core_hbm, core_ref), (local_hbm, local_ref))
+        )
+    ]
+    for field in fields:
+        field.start()
 
     def weights_of(t):
         i = lax.broadcasted_iota(jnp.int32, (6 * LANES, 2 * LANES), 0) + 2 * LANES * (t - 1)
@@ -192,11 +152,69 @@
     over = jnp.where(plane == 3, 0.0, jnp.where(q - p == 1, -0.5, 0.0))
     normal[...] = (under + over).astype(jnp.bfloat16)
 
+    last = bands - 1
+    rows = 4 * tiles
+    last_rows = rows // LAST_PIECES
+
+    def slots(b):
+        if b < last:
+            return [(b, pl.ds(0, rows), b)]
+        return [(b, pl.ds(k * last_rows, last_rows), last + k) for k in range(LAST_PIECES)]
+
+    def up_copy(slot):
+        b, r, s = slot
+        return pltpu.make_async_remote_copy(
+            send_up.at[b, r], from_below.at[b, r], up_send.at[s], up_recv.at[s],
+            device_id=above, device_id_type=MESH,
+        )
+
+    def down_copy(slot):
+        b, r, s = slot
+        return pltpu.make_async_remote_copy(
+            send_down.at[b, r], from_above.at[b, r], down_send.at[s], down_recv.at[s],
+            device_id=below, device_id_type=MESH,
+        )
+
+    def extract(b):
+        for c in range(4):
+            load(b, c).wait()
+        n = ROWS_PER_STEP
+
+        def step(i, carry):
+            j = i * n
+            values = xb[b, pl.ds(2 + j, n)].reshape(n * 16, LANES)
+            stage[...] = values.astype(jnp.float32)
+            r = pl.multiple_of(4 * j, 4 * n)
+            send_up[b, pl.ds(r, 4 * n)] = stage[pl.ds(3, 4 * n, stride=4)].astype(jnp.bfloat16)
+            send_down[b, pl.ds(r, 4 * n)] = stage[pl.ds(0, 4 * n, stride=4)].astype(jnp.bfloat16)
+            return carry
+
+        lax.fori_loop(0, tiles // n, step, 0)
+
+    def send(b):
+        for slot in slots(b):
+
+            @pl.when(has_above)
+            def _():
+                up_copy(slot).start()
+
+            @pl.when(has_below)
+            def _():
+                down_copy(slot).start()
+
+    for b in range(EARLY + 1):
+        extract(b)
+
     pl.semaphore_wait(
         barrier, 3 + has_above.astype(jnp.int32) + has_below.astype(jnp.int32)
     )
     for b in range(EARLY):
         send(b)
+    for b in range(EARLY + 1, bands):
+        extract(b)
+
+    for field in fields:
+        field.wait()
 
     low = lax.broadcasted_iota(jnp.int32, (8, LANES), 0) < 4
     weights = [
@@ -520,14 +538,17 @@
     local = local_potential.reshape(planes, tiles, LANES).transpose(1, 0, 2)
     dma = pltpu.SemaphoreType.DMA
     in_vmem = pl.BlockSpec(memory_space=pltpu.VMEM)
-    in_smem = pl.BlockSpec(memory_space=pltpu.SMEM)
     anywhere = pl.BlockSpec(memory_space=pl.ANY)
     applied = pl.pallas_call(
         functools.partial(halo_kernel, bands, tiles),
         out_shape=pltpu.VMEM((bands, tiles, parts * planes, LANES), bf16),
-        in_specs=[in_smem, in_smem, anywhere, in_vmem, in_vmem],
+        in_specs=[anywhere] * 5,
         out_specs=in_vmem,
         scratch_shapes=[
+            pltpu.SMEM((bands,), jnp.int32),
+            pltpu.SMEM((bands,), jnp.int32),
+            pltpu.VMEM((tiles, planes, LANES), f32),
+            pltpu.VMEM((tiles, planes, LANES), f32),
             pltpu.VMEM((bands, tiles + 4, parts * planes, LANES), bf16),
             pltpu.VMEM((bands, 4 * tiles, LANES), bf16),
             pltpu.VMEM((bands, 4 * tiles, LANES), bf16),
@@ -546,6 +567,7 @@
             pltpu.VMEM((tiles, 4, 8, LANES), f32),
             dma((bands, 4)),
             dma((2, 4)),
+            dma((4,)),
             dma((copies,)),
             dma((copies,)),
             dma((copies,)),

time: 72.4 us -> 68.7 us (0.949)
  Pallas kernels: 72.2 us -> 68.6 us
    pallas_call x1, Pallas kernels: 68.4 us -> 64.7 us  [shards(): pl.pallas_call(functools.partial(halo_kernel, bands, tiles), out_shape=pl...]
where the time goes in v3:
time: 68.7 us; the launch traced here: 68.6 us
  Pallas kernels  68.6 us (100%)
    pallas_call x1, Pallas kernels, shards(): pl.pallas_call(functools.partial(halo_kernel, bands, tiles), out_shape=pl...  64.7 us
    pallas_call x1, Pallas kernels, shards(): pl.pallas_call(functools.partial(write_kernel, bands), out_shape=jax.Shap...  3.87 us

profile of v3, /device:TPU:96, one launch (start us, length us, event | category | flops | bytes accessed | tf_op | source)
XLA Modules:
  0.0 68.6 jit_solution(13117967209689516818)
XLA Ops:
  0.0 64.7 %shard_map.55.in_ref = bf16[8,288,16,128]{3,2,1,0:T(8,128)(2,1)S(1)} custom-call(s32[8]{0:T(128)} %kpt_hbm.1, s32[8]{0:T(128)} %occ_hbm.1, bf16[8,4,288,4,128]{4,3,2,1,0:T(4,128)(2,1)} %bitcast.12, f32[288,4,128]{2,1,0:T(4,128)} %bitcast.13, f32[288,4,128]{2,1,0:T(4,128)} %bitcast.14), custom_call_target="tpu_custom_call" | custom-call | tf_op jit(solution)/shard_map/pallas_call | solution.py:542
  64.7 3.9 %shard_map.56 = bf16[8,4,288,4,128]{4,3,2,1,0:T(4,128)(2,1)} custom-call(bf16[8,288,16,128]{3,2,1,0:T(8,128)(2,1)S(1)} %shard_map.55.in_ref), custom_call_target="tpu_custom_call" | custom-call | tf_op jit(solution)/shard_map/pallas_call | solution.py:588

commit v4 on v3

--- a/solution.py
+++ b/solution.py
@@ -18,6 +18,7 @@
 MIX_STEP = 8
 SUM_STEP = 6
 POTENTIAL_STEP = 6
+DIRECT_PIECES = 2
 EARLY = 2
 
 
@@ -87,7 +88,7 @@
     inner = jnp.logical_not(edge)
     half = tiles // 2
     piece = half // DENSITY_PIECES
-    direct = DENSITY_PIECES // 2
+    direct = DIRECT_PIECES
 
     barrier = pltpu.get_barrier_semaphore()
 
@@ -300,28 +301,6 @@
             def _():
                 cross_copy(k).start()
 
-    order = list(range(direct, DENSITY_PIECES)) + list(range(direct))
-    for n, k in enumerate(order):
-        lax.fori_loop(k * piece // SUM_STEP, (k + 1) * piece // SUM_STEP, sum_half, 0)
-        if n:
-            cross_start(order[n - 1])
-    send(EARLY)
-    cross_start(order[-1])
-    for b in range(EARLY + 1, bands):
-        send(b)
-
-    for end in range(2):
-        for c in range(4):
-            wrap(end, c).wait()
-
-    @pl.when(jnp.logical_not(has_below))
-    def _():
-        from_below[...] = jnp.zeros_like(from_below)
-
-    @pl.when(jnp.logical_not(has_above))
-    def _():
-        from_above[...] = jnp.zeros_like(from_above)
-
     group = 8
 
     def kinetic(b):
@@ -356,7 +335,29 @@
 
         lax.fori_loop(0, tiles // (6 * group), step, 0)
 
+    for end in range(2):
+        for c in range(4):
+            wrap(end, c).wait()
+
+    order = list(range(direct, DENSITY_PIECES)) + list(range(direct))
+    for n, k in enumerate(order):
+        lax.fori_loop(k * piece // SUM_STEP, (k + 1) * piece // SUM_STEP, sum_half, 0)
+        if n:
+            cross_start(order[n - 1])
+    send(EARLY)
     kinetic(0)
+    cross_start(order[-1])
+    for b in range(EARLY + 1, bands):
+        send(b)
+
+    @pl.when(jnp.logical_not(has_below))
+    def _():
+        from_below[...] = jnp.zeros_like(from_below)
+
+    @pl.when(jnp.logical_not(has_above))
+    def _():
+        from_above[...] = jnp.zeros_like(from_above)
+
     for k in range(direct, DENSITY_PIECES):
         kinetic(k - direct + 1)
 
@@ -530,7 +531,7 @@
     tiles = cells // LANES
     half = tiles // 2
     piece = half // DENSITY_PIECES
-    relayed = DENSITY_PIECES - DENSITY_PIECES // 2
+    relayed = DENSITY_PIECES - DIRECT_PIECES
     copies = bands - 1 + LAST_PIECES
     bf16, f32 = jnp.bfloat16, jnp.float32
     view = spinors.reshape(bands, parts, planes, tiles, LANES).transpose(0, 1, 3, 2, 4)

time: 68.7 us -> 68.7 us (level)
  no operation moved by 1% of the time
where the time goes in v4:
time: 68.7 us; the launch traced here: 68.6 us
  Pallas kernels  68.6 us (100%)
    pallas_call x1, Pallas kernels, shards(): pl.pallas_call(functools.partial(halo_kernel, bands, tiles), out_shape=pl...  64.7 us
    pallas_call x1, Pallas kernels, shards(): pl.pallas_call(functools.partial(write_kernel, bands), out_shape=jax.Shap...  3.87 us

profile of v4, /device:TPU:96, one launch (start us, length us, event | category | flops | bytes accessed | tf_op | source)
XLA Modules:
  0.0 68.6 jit_solution(10860420546930466220)
XLA Ops:
  0.0 64.7 %shard_map.55.in_ref = bf16[8,288,16,128]{3,2,1,0:T(8,128)(2,1)S(1)} custom-call(s32[8]{0:T(128)} %kpt_hbm.1, s32[8]{0:T(128)} %occ_hbm.1, bf16[8,4,288,4,128]{4,3,2,1,0:T(4,128)(2,1)} %bitcast.12, f32[288,4,128]{2,1,0:T(4,128)} %bitcast.13, f32[288,4,128]{2,1,0:T(4,128)} %bitcast.14), custom_call_target="tpu_custom_call" | custom-call | tf_op jit(solution)/shard_map/pallas_call | solution.py:543
  64.7 3.9 %shard_map.56 = bf16[8,4,288,4,128]{4,3,2,1,0:T(4,128)(2,1)} custom-call(bf16[8,288,16,128]{3,2,1,0:T(8,128)(2,1)S(1)} %shard_map.55.in_ref), custom_call_target="tpu_custom_call" | custom-call | tf_op jit(solution)/shard_map/pallas_call | solution.py:589
